TPU v7x, 32 devices: a whole 2x2x4 slice. The times are simulated.
32 devices in a mesh: outer: 8 (over y, x, core), inner: 4 (over z).
Axes of the slice: x: 2, y: 2, z: 4, core: 2. Of those that a mesh axis runs over, the one named last changes fastest.
Arguments:
- query_image: bfloat16 [2048, 1024], P(('outer', 'inner')), may hold values from -6 to 6
- key_image: bfloat16 [2048, 1024], P(('outer', 'inner')), may hold values from -6 to 6
- value_image: bfloat16 [2048, 1024], P(('outer', 'inner')), may hold values from -6 to 6
- attended_image: bfloat16 [2048, 1024], P(('outer', 'inner')), may hold values from -6 to 6
- upstream_image: bfloat16 [2048, 1024], P(('outer', 'inner')), may hold values from -128 to 128
- logsum_image: float32 [2048, 8], P(('outer', 'inner')), may hold values from 8.6 to 9.4
- query_text: bfloat16 [512, 1024], P(None, 'outer'), may hold values from -6 to 6
- key_text: bfloat16 [512, 1024], P(None, 'outer'), may hold values from -6 to 6
- value_text: bfloat16 [512, 1024], P(None, 'outer'), may hold values from -6 to 6
- attended_text: bfloat16 [512, 1024], P(None, 'outer'), may hold values from -6 to 6
- upstream_text: bfloat16 [512, 1024], P(None, 'outer'), may hold values from -128 to 128
- logsum_text: float32 [512, 8], P(None, 'outer'), may hold values from 8.6 to 9.4
Outputs:
- grad_query_image: bfloat16 [2048, 1024], P(('outer', 'inner'))
- grad_key_image: bfloat16 [2048, 1024], P(('outer', 'inner'))
- grad_value_image: bfloat16 [2048, 1024], P(('outer', 'inner'))
- grad_query_text: bfloat16 [512, 1024], P('inner', 'outer')
- grad_key_text: bfloat16 [512, 1024], P('inner', 'outer')
- grad_value_text: bfloat16 [512, 1024], P('inner', 'outer')
All inputs are finite; a program needn't handle non-finite values.
Results may differ from a plain program's by a relative error of at most 0.0055.
Values may be sent and summed in bfloat16 or wider, within the bound.
A program may use at most 64 MiB of HBM per device.

v0:
```python
import math
import jax
import jax.numpy as jnp
from jax import lax
from jax.sharding import PartitionSpec as P

HEAD_DIM = 128


def across_rows(left, right):
    return lax.dot_general(
        left, right, (((1,), (1,)), ((), ())), preferred_element_type=jnp.float32
    )


def down_rows(left, right):
    return lax.dot_general(
        left, right, (((0,), (0,)), ((), ())), preferred_element_type=jnp.float32
    )


def weights_and_mixed(queries, upstream, log_sums, deltas, keys, values):
    scores = across_rows(queries, keys) * HEAD_DIM ** (-0.5)
    weights = jnp.exp(scores - log_sums)
    slopes = across_rows(upstream, values)
    mixed = weights * (slopes - deltas)
    return (weights.astype(jnp.bfloat16), mixed.astype(jnp.bfloat16))


def query_side(mixed_half, keys):
    return jnp.dot(mixed_half, keys, preferred_element_type=jnp.float32) * HEAD_DIM ** (-0.5)


def key_side(weights_half, mixed_half, queries, upstream):
    grad_values = down_rows(weights_half, upstream)
    grad_keys = down_rows(mixed_half, queries) * HEAD_DIM ** (-0.5)
    return (grad_keys, grad_values)


def shards(
    query_image,
    key_image,
    value_image,
    attended_image,
    upstream_image,
    logsum_image,
    query_text,
    key_text,
    value_text,
    attended_text,
    upstream_text,
    logsum_text,
):
    queries, keys, values, upstream, attended = (
        lax.all_to_all(query_image, "outer", split_axis=1, concat_axis=0, tiled=True),
        lax.all_to_all(key_image, "outer", split_axis=1, concat_axis=0, tiled=True),
        lax.all_to_all(value_image, "outer", split_axis=1, concat_axis=0, tiled=True),
        lax.all_to_all(upstream_image, "outer", split_axis=1, concat_axis=0, tiled=True),
        lax.all_to_all(attended_image, "outer", split_axis=1, concat_axis=0, tiled=True),
    )
    log_sums = lax.all_to_all(logsum_image, "outer", split_axis=1, concat_axis=0, tiled=True)
    deltas = jnp.sum(
        upstream.astype(jnp.float32) * attended.astype(jnp.float32), axis=1, keepdims=True
    )
    text_deltas = jnp.sum(
        upstream_text.astype(jnp.float32) * attended_text.astype(jnp.float32), axis=1, keepdims=True
    )
    weights_half, mixed_half = weights_and_mixed(
        queries, upstream, log_sums, deltas, key_text, value_text
    )
    grad_query_near = query_side(mixed_half, key_text)
    text_key_first, text_value_first = key_side(weights_half, mixed_half, queries, upstream)
    weights_half, mixed_half = weights_and_mixed(
        query_text, upstream_text, logsum_text, text_deltas, keys, values
    )
    text_query_first = query_side(mixed_half, keys)
    grad_key_near, grad_value_near = key_side(weights_half, mixed_half, query_text, upstream_text)
    share = query_text.shape[0] // lax.axis_size("inner")
    first_row = lax.axis_index("inner") * share

    def text_rows(matrix):
        return lax.dynamic_slice_in_dim(matrix, first_row, share, 0)

    own_queries = text_rows(query_text)
    own_upstream = text_rows(upstream_text)
    weights_half, mixed_half = weights_and_mixed(
        own_queries,
        own_upstream,
        text_rows(logsum_text),
        text_rows(text_deltas),
        key_text,
        value_text,
    )
    text_query_rows = query_side(mixed_half, key_text)
    text_key_second, text_value_second = key_side(
        weights_half, mixed_half, own_queries, own_upstream
    )
    text_query = lax.dynamic_update_slice_in_dim(
        text_query_first, text_rows(text_query_first) + text_query_rows, first_row, 0
    )
    zero_rows = jnp.zeros(queries.shape, jnp.float32)
    whole_keys, whole_values = (
        lax.all_gather(keys, "inner", axis=0, tiled=True),
        lax.all_gather(values, "inner", axis=0, tiled=True),
    )
    key_count = whole_keys.shape[0]
    size = math.gcd(key_count, 1024)
    count = key_count // size
    stacked_keys = whole_keys.reshape(count, size, whole_keys.shape[1])
    stacked_values = whole_values.reshape(count, size, whole_values.shape[1])

    def key_block(carry, block):
        weights_block, mixed_block = weights_and_mixed(
            queries, upstream, log_sums, deltas, block[0], block[1]
        )
        terms = key_side(weights_block, mixed_block, queries, upstream)
        return (carry + query_side(mixed_block, block[0]), terms)

    grad_query_far, stacked_terms = lax.scan(key_block, zero_rows, (stacked_keys, stacked_values))
    key_terms = stacked_terms[0].reshape(key_count, whole_keys.shape[1])
    value_terms = stacked_terms[1].reshape(key_count, whole_keys.shape[1])
    grad_key_far, grad_value_far = (
        lax.psum_scatter(key_terms, "inner", scatter_dimension=0, tiled=True),
        lax.psum_scatter(value_terms, "inner", scatter_dimension=0, tiled=True),
    )
    head_grads = (
        (grad_query_near + grad_query_far).astype(jnp.bfloat16),
        (grad_key_near + grad_key_far).astype(jnp.bfloat16),
        (grad_value_near + grad_value_far).astype(jnp.bfloat16),
    )
    image_query, image_key, image_value = (
        lax.all_to_all(head_grads[0], "outer", split_axis=0, concat_axis=1, tiled=True),
        lax.all_to_all(head_grads[1], "outer", split_axis=0, concat_axis=1, tiled=True),
        lax.all_to_all(head_grads[2], "outer", split_axis=0, concat_axis=1, tiled=True),
    )
    summed_query, summed_key, summed_value = (
        lax.psum_scatter(text_query, "inner", scatter_dimension=0, tiled=True),
        lax.psum_scatter(
            text_key_first + text_key_second, "inner", scatter_dimension=0, tiled=True
        ),
        lax.psum_scatter(
            text_value_first + text_value_second, "inner", scatter_dimension=0, tiled=True
        ),
    )
    return (
        image_query,
        image_key,
        image_value,
        summed_query.astype(jnp.bfloat16),
        summed_key.astype(jnp.bfloat16),
        summed_value.astype(jnp.bfloat16),
    )


def solution(mesh):
    in_specs = (
        P(("outer", "inner"), None),
        P(("outer", "inner"), None),
        P(("outer", "inner"), None),
        P(("outer", "inner"), None),
        P(("outer", "inner"), None),
        P(("outer", "inner"), None),
        P(None, "outer"),
        P(None, "outer"),
        P(None, "outer"),
        P(None, "outer"),
        P(None, "outer"),
        P(None, "outer"),
    )
    out_specs = (
        P(("outer", "inner"), None),
        P(("outer", "inner"), None),
        P(("outer", "inner"), None),
        P("inner", "outer"),
        P("inner", "outer"),
        P("inner", "outer"),
    )
    return jax.shard_map(shards, mesh=mesh, in_specs=in_specs, out_specs=out_specs, check_vma=False)
```

profile of v0, /device:TPU:0, one launch (start us, length us, event | category | flops | bytes accessed | tf_op | source)
XLA Modules:
  0.0 203.6 jit_solution(8097618321480912621)
XLA Ops:
  7.2 5.3 %all-to-all-start.1 = ((f32[64,8,1]{0,2,1:T(1,128)}), f32[64,8,1]{0,2,1:T(1,128)S(1)}, u32[]{:S(2)}, u32[]{:S(2)}) async-start(f32[64,8,1]{0,2,1:T(1,128)} %bitcast.168), calls=%async_computation.1 | async-start | bytes 8192 | tf_op jit(solution)/shard_map/all_to_all | solution.py:61
  12.6 1.6 copy_bitcast_fusion.4
  14.2 1.6 copy_bitcast_fusion.7
  15.7 1.6 copy_bitcast_fusion.3
  17.4 1.1 multiply_reduce_fusion
  18.5 0.7 fusion.52
  19.2 1.0 fusion.30
  20.2 1.1 fusion.34
  21.3 0.7 copy_bitcast_fusion.6
  22.0 4.2 %all-to-all-start.4 = ((bf16[64,8,128]{2,0,1:T(8,128)(2,1)}), bf16[64,8,128]{2,0,1:T(8,128)(2,1)S(1)}, u32[]{:S(2)}, u32[]{:S(2)}) async-start(bf16[64,8,128]{2,0,1:T(8,128)(2,1)} %copy_bitcast_fusion.4), calls=%async_computation.4 | async-start | bytes 262144 | tf_op jit(solution)/shard_map/all_to_all | solution.py:56
  26.2 0.7 copy_bitcast_fusion.5
  27.1 4.6 %all-to-all-done.4 = bf16[64,8,128]{2,0,1:T(8,128)(2,1)S(1)} async-done(((bf16[64,8,128]{2,0,1:T(8,128)(2,1)}), bf16[64,8,128]{2,0,1:T(8,128)(2,1)S(1)}, u32[]{:S(2)}, u32[]{:S(2)}) %all-to-all-start.4) | async-done | bytes 131104 | tf_op jit(solution)/shard_map/all_to_all | solution.py:56
  31.7 3.4 %all-to-all-start.5 = ((bf16[64,8,128]{2,0,1:T(8,128)(2,1)}), bf16[64,8,128]{2,0,1:T(8,128)(2,1)S(1)}, u32[]{:S(2)}, u32[]{:S(2)}) async-start(bf16[64,8,128]{2,0,1:T(8,128)(2,1)} %copy_bitcast_fusion.3), calls=%async_computation.5 | async-start | bytes 262144 | tf_op jit(solution)/shard_map/all_to_all | solution.py:57
  35.4 5.1 %all-to-all-done.5 = bf16[64,8,128]{2,0,1:T(8,128)(2,1)S(1)} async-done(((bf16[64,8,128]{2,0,1:T(8,128)(2,1)}), bf16[64,8,128]{2,0,1:T(8,128)(2,1)S(1)}, u32[]{:S(2)}, u32[]{:S(2)}) %all-to-all-start.5) | async-done | bytes 131104 | tf_op jit(solution)/shard_map/all_to_all | solution.py:57
  40.5 3.4 %all-to-all-start.2 = ((bf16[64,8,128]{2,0,1:T(8,128)(2,1)}), bf16[64,8,128]{2,0,1:T(8,128)(2,1)S(1)}, u32[]{:S(2)}, u32[]{:S(2)}) async-start(bf16[64,8,128]{2,0,1:T(8,128)(2,1)} %copy_bitcast_fusion.6), calls=%async_computation.2 | async-start | bytes 262144 | tf_op jit(solution)/shard_map/all_to_all | solution.py:58
  44.2 0.8 copy-done.7
  45.3 4.0 %all-to-all-done.2 = bf16[64,8,128]{2,0,1:T(8,128)(2,1)S(1)} async-done(((bf16[64,8,128]{2,0,1:T(8,128)(2,1)}), bf16[64,8,128]{2,0,1:T(8,128)(2,1)S(1)}, u32[]{:S(2)}, u32[]{:S(2)}) %all-to-all-start.2) | async-done | bytes 131104 | tf_op jit(solution)/shard_map/all_to_all | solution.py:58
  49.3 3.4 %all-to-all-start.3 = ((bf16[64,8,128]{2,0,1:T(8,128)(2,1)}), bf16[64,8,128]{2,0,1:T(8,128)(2,1)S(1)}, u32[]{:S(2)}, u32[]{:S(2)}) async-start(bf16[64,8,128]{2,0,1:T(8,128)(2,1)} %copy_bitcast_fusion.5), calls=%async_computation.3 | async-start | bytes 262144 | tf_op jit(solution)/shard_map/all_to_all | solution.py:59
  52.9 5.2 %all-to-all-done.3 = bf16[64,8,128]{2,0,1:T(8,128)(2,1)S(1)} async-done(((bf16[64,8,128]{2,0,1:T(8,128)(2,1)}), bf16[64,8,128]{2,0,1:T(8,128)(2,1)S(1)}, u32[]{:S(2)}, u32[]{:S(2)}) %all-to-all-start.3) | async-done | bytes 131104 | tf_op jit(solution)/shard_map/all_to_all | solution.py:59
  58.1 3.4 %all-to-all-start = ((bf16[64,8,128]{2,0,1:T(8,128)(2,1)}), bf16[64,8,128]{2,0,1:T(8,128)(2,1)S(1)}, u32[]{:S(2)}, u32[]{:S(2)}) async-start(bf16[64,8,128]{2,0,1:T(8,128)(2,1)} %copy_bitcast_fusion.7), calls=%async_computation | async-start | bytes 262144 | tf_op jit(solution)/shard_map/all_to_all | solution.py:55
  62.3 4.6 %all-to-all-done = bf16[64,8,128]{2,0,1:T(8,128)(2,1)S(1)} async-done(((bf16[64,8,128]{2,0,1:T(8,128)(2,1)}), bf16[64,8,128]{2,0,1:T(8,128)(2,1)S(1)}, u32[]{:S(2)}, u32[]{:S(2)}) %all-to-all-start) | async-done | bytes 131104 | tf_op jit(solution)/shard_map/all_to_all | solution.py:55
  67.6 19.9 %all_gather.6 = bf16[2048,128]{1,0:T(8,128)(2,1)S(1)} all-gather(bf16[512,128]{1,0:T(8,128)(2,1)S(1)} %bitcast.158), channel_id=1, replica_groups=mesh['outer'=8,'inner'=4] {'inner'}, dimensions={0}, use_global_device_ids=true | all-gather | bytes 655360 | tf_op jit(solution)/shard_map/all_gather | solution.py:103
  87.9 0.9 fusion.27
  88.9 17.1 %all_gather.7 = bf16[2048,128]{1,0:T(8,128)(2,1)} all-gather(bf16[512,128]{1,0:T(8,128)(2,1)S(1)} %bitcast.160), channel_id=1, replica_groups=mesh['outer'=8,'inner'=4] {'inner'}, dimensions={0}, use_global_device_ids=true | all-gather | bytes 655360 | tf_op jit(solution)/shard_map/all_gather | solution.py:104
  106.4 0.9 convolution_add_fusion
  107.4 13.6 %while.15 = (s32[]{:T(128)}, f32[512,128]{1,0:T(8,128)}, f32[2,1024,128]{2,1,0:T(8,128)}, f32[2,1024,128]{2,1,0:T(8,128)}, bf16[2,1024,128]{2,1,0:T(8,128)(2,1)S...) while((s32[]{:T(128)}, f32[512,128]{1,0:T(8,128)}, ...), condition=%wide.region_2.3_spmd.clone, body=%wide.region_1.0_spmd.clone.sunk | while | flops 675610624 | bytes 27007272 | solution.py:119
  108.6 0.6 multiply_convert_fusion.2
  109.2 2.2 %fusion.116 = f32[512,128]{1,0:T(8,128)} fusion(bf16[1024,512]{1,0:T(8,128)(2,1)S(1)} %multiply_convert_fusion.2, f32[512,128]{1,0:T(8,128)} %get-tuple-element.190, bf16[2,1024,128]{2,1,0:T(8,128)(2,1)} %copy-done.1, s32[]{:T(128)S(6)} %copy.62, pred[]{:T(512)S(6)} %compare.3), kind=kOutput, calls=%fused_computation.9.clone.1 | convolution fusion | flops 134414336 | bytes 1835013 | tf_op jit(solution)/shard_map/while/body/eval_jaxpr/dot_general | solution.py:31
  111.4 1.3 fusion.117
  113.2 1.0 copy-done.15
  115.4 0.5 multiply_convert_fusion.2
  116.0 2.3 %fusion.116 = f32[512,128]{1,0:T(8,128)} fusion(bf16[1024,512]{1,0:T(8,128)(2,1)S(1)} %multiply_convert_fusion.2, f32[512,128]{1,0:T(8,128)} %get-tuple-element.190, bf16[2,1024,128]{2,1,0:T(8,128)(2,1)} %copy-done.1, s32[]{:T(128)S(6)} %copy.62, pred[]{:T(512)S(6)} %compare.3), kind=kOutput, calls=%fused_computation.9.clone.1 | convolution fusion | flops 134414336 | bytes 1835013 | tf_op jit(solution)/shard_map/while/body/eval_jaxpr/dot_general | solution.py:31
  118.3 1.2 fusion.117
  120.0 1.0 copy-done.15
  122.4 7.9 %all_to_all.165 = bf16[8,64,128]{2,1,0:T(8,128)(2,1)S(1)} all-to-all(bf16[8,64,128]{2,1,0:T(8,128)(2,1)S(1)} %bitcast.163), channel_id=1, replica_groups=mesh['outer'=8,'inner'=4] {'outer'}, dimensions={0} | all-to-all | bytes 262144 | tf_op jit(solution)/shard_map/all_to_all | solution.py:132
  130.3 0.7 copy_bitcast_fusion.2
  131.0 1.5 convert_element_type.70
  132.4 1.5 convert_element_type.71
  133.9 1.5 convert_element_type.74
  135.3 22.0 %reduce-scatter.6.cloned.1.call-done = f32[512,128]{1,0:T(8,128)} async-done(((f32[2048,128]{1,0:T(8,128)}), f32[512,128]{1,0:T(8,128)}) %reduce-scatter.6.cloned.1.call-update) | async-done | bytes 262160 | tf_op jit(solution)/shard_map/reduce_scatter | solution.py:123
  157.3 2.0 fusion.35
  159.3 3.6 %all-to-all-start.7 = ((bf16[8,64,128]{2,1,0:T(8,128)(2,1)}), bf16[8,64,128]{2,1,0:T(8,128)(2,1)S(1)}, u32[]{:S(2)}, u32[]{:S(2)}) async-start(bf16[8,64,128]{2,1,0:T(8,128)(2,1)} %bitcast.21), calls=%async_computation.8 | async-start | bytes 262144 | tf_op jit(solution)/shard_map/all_to_all | solution.py:133
  162.9 22.3 %reduce-scatter.8.cloned.1.call-done = f32[512,128]{1,0:T(8,128)} async-done(((f32[2048,128]{1,0:T(8,128)}), f32[512,128]{1,0:T(8,128)}) %reduce-scatter.8.cloned.1.call-update) | async-done | bytes 262160 | tf_op jit(solution)/shard_map/reduce_scatter | solution.py:124
  185.3 2.0 fusion.33
  187.2 3.6 %all-to-all-start.8 = ((bf16[8,64,128]{2,1,0:T(8,128)(2,1)}), bf16[8,64,128]{2,1,0:T(8,128)(2,1)S(1)}, u32[]{:S(2)}, u32[]{:S(2)}) async-start(bf16[8,64,128]{2,1,0:T(8,128)(2,1)} %bitcast.24), calls=%async_computation.10 | async-start | bytes 262144 | tf_op jit(solution)/shard_map/all_to_all | solution.py:134
  190.9 0.7 copy_bitcast_fusion.1
  191.5 4.8 %all-to-all-done.8 = bf16[8,64,128]{2,1,0:T(8,128)(2,1)S(1)} async-done(((bf16[8,64,128]{2,1,0:T(8,128)(2,1)}), bf16[8,64,128]{2,1,0:T(8,128)(2,1)S(1)}, u32[]{:S(2)}, u32[]{:S(2)}) %all-to-all-start.8) | async-done | bytes 131104 | tf_op jit(solution)/shard_map/all_to_all | solution.py:134
  196.4 0.7 copy_bitcast_fusion
  (89 shorter events, 8.5 us)
Async XLA Ops:
  7.2 12.0 %copy-start = (bf16[512,128]{1,0:T(8,128)(2,1)S(1)}, bf16[512,128]{1,0:T(8,128)(2,1)}, u32[]{:S(2)}) copy-start(bf16[512,128]{1,0:T(8,128)(2,1)} %param.21) | copy-start | bytes 393220
  7.2 27.9 %copy-start.21 = (f32[512,1]{0,1:T(1,128)S(1)}, f32[512,1]{0,1:T(1,128)}, u32[]{:S(2)}) copy-start(f32[512,1]{0,1:T(1,128)} %param.25) | copy-start | bytes 6148
  7.2 27.9 %copy-start.16 = (bf16[512,128]{1,0:T(8,128)(2,1)S(1)}, bf16[512,128]{1,0:T(8,128)(2,1)}, u32[]{:S(2)}) copy-start(bf16[512,128]{1,0:T(8,128)(2,1)} %param.20) | copy-start | bytes 393220
  7.2 14.1 %copy-start.19 = (bf16[64,1024]{1,0:T(8,128)(2,1)S(1)}, bf16[64,1024]{1,0:T(8,128)(2,1)}, u32[]{:S(2)}) copy-start(bf16[64,1024]{1,0:T(8,128)(2,1)} %param.18) | copy-start | bytes 393220
  7.2 19.0 %copy-start.20 = (bf16[64,1024]{1,0:T(8,128)(2,1)S(1)}, bf16[64,1024]{1,0:T(8,128)(2,1)}, u32[]{:S(2)}) copy-start(bf16[64,1024]{1,0:T(8,128)(2,1)} %param.17) | copy-start | bytes 393220
  7.2 14.8 %all-to-all-start.1 = ((f32[64,8,1]{0,2,1:T(1,128)}), f32[64,8,1]{0,2,1:T(1,128)S(1)}, u32[]{:S(2)}, u32[]{:S(2)}) async-start(f32[64,8,1]{0,2,1:T(1,128)} %bitcast.168), calls=%async_computation.1 | async-start | bytes 8192 | tf_op jit(solution)/shard_map/all_to_all | solution.py:61
  15.7 28.2 %copy-start.11 = (bf16[512,128]{1,0:T(8,128)(2,1)S(1)}, bf16[512,128]{1,0:T(8,128)(2,1)}, u32[]{:S(2)}) copy-start(bf16[512,128]{1,0:T(8,128)(2,1)} %param.24) | copy-start | bytes 393220
  22.0 9.7 %all-to-all-start.4 = ((bf16[64,8,128]{2,0,1:T(8,128)(2,1)}), bf16[64,8,128]{2,0,1:T(8,128)(2,1)S(1)}, u32[]{:S(2)}, u32[]{:S(2)}) async-start(bf16[64,8,128]{2,0,1:T(8,128)(2,1)} %copy_bitcast_fusion.4), calls=%async_computation.4 | async-start | bytes 262144 | tf_op jit(solution)/shard_map/all_to_all | solution.py:56
  31.7 8.8 %all-to-all-start.5 = ((bf16[64,8,128]{2,0,1:T(8,128)(2,1)}), bf16[64,8,128]{2,0,1:T(8,128)(2,1)S(1)}, u32[]{:S(2)}, u32[]{:S(2)}) async-start(bf16[64,8,128]{2,0,1:T(8,128)(2,1)} %copy_bitcast_fusion.3), calls=%async_computation.5 | async-start | bytes 262144 | tf_op jit(solution)/shard_map/all_to_all | solution.py:57
  35.4 22.7 %copy-start.4 = (f32[512,512]{1,0:T(8,128)}, f32[512,512]{1,0:T(8,128)S(1)}, u32[]{:S(2)}) copy-start(f32[512,512]{1,0:T(8,128)S(1)} %fusion.23) | copy-start | bytes 3145732
  40.5 8.8 %all-to-all-start.2 = ((bf16[64,8,128]{2,0,1:T(8,128)(2,1)}), bf16[64,8,128]{2,0,1:T(8,128)(2,1)S(1)}, u32[]{:S(2)}, u32[]{:S(2)}) async-start(bf16[64,8,128]{2,0,1:T(8,128)(2,1)} %copy_bitcast_fusion.6), calls=%async_computation.2 | async-start | bytes 262144 | tf_op jit(solution)/shard_map/all_to_all | solution.py:58
  44.2 0.8 copy-start.7
  45.0 22.3 %copy-start.18 = (bf16[512,128]{1,0:T(8,128)(2,1)S(1)}, bf16[512,128]{1,0:T(8,128)(2,1)}, u32[]{:S(2)}) copy-start(bf16[512,128]{1,0:T(8,128)(2,1)} %param.22) | copy-start | bytes 393220
  49.3 8.8 %all-to-all-start.3 = ((bf16[64,8,128]{2,0,1:T(8,128)(2,1)}), bf16[64,8,128]{2,0,1:T(8,128)(2,1)S(1)}, u32[]{:S(2)}, u32[]{:S(2)}) async-start(bf16[64,8,128]{2,0,1:T(8,128)(2,1)} %copy_bitcast_fusion.5), calls=%async_computation.3 | async-start | bytes 262144 | tf_op jit(solution)/shard_map/all_to_all | solution.py:59
  52.9 8.9 %copy-start.13 = (f32[512,128]{1,0:T(8,128)}, f32[512,128]{1,0:T(8,128)S(1)}, u32[]{:S(2)}) copy-start(f32[512,128]{1,0:T(8,128)S(1)} %fusion.38) | copy-start | bytes 786436
  58.1 8.8 %all-to-all-start = ((bf16[64,8,128]{2,0,1:T(8,128)(2,1)}), bf16[64,8,128]{2,0,1:T(8,128)(2,1)S(1)}, u32[]{:S(2)}, u32[]{:S(2)}) async-start(bf16[64,8,128]{2,0,1:T(8,128)(2,1)} %copy_bitcast_fusion.7), calls=%async_computation | async-start | bytes 262144 | tf_op jit(solution)/shard_map/all_to_all | solution.py:55
  61.5 69.4 %reduce-scatter.10.cloned.1.call-start = ((), (), s32[]{:S(2)}) async-start(), calls=%async_computation.16 | async-start | bytes 327680 | tf_op jit(solution)/shard_map/reduce_scatter | solution.py:137
  62.3 70.2 %reduce-scatter.12.cloned.1.call-start = ((), (), s32[]{:S(2)}) async-start(), calls=%async_computation.17 | async-start | bytes 327680 | tf_op jit(solution)/shard_map/reduce_scatter | solution.py:138
  67.6 38.7 %copy-start.9 = (bf16[512,512]{1,0:T(8,128)(2,1)}, bf16[512,512]{1,0:T(8,128)(2,1)S(1)}, u32[]{:S(2)}) copy-start(bf16[512,512]{1,0:T(8,128)(2,1)S(1)} %fusion.26) | copy-start | bytes 1572868
  88.8 45.0 %reduce-scatter.14.cloned.1.call-start = ((), (), s32[]{:S(2)}) async-start(), calls=%async_computation.18 | async-start | bytes 327680 | tf_op jit(solution)/shard_map/reduce_scatter | solution.py:141
  107.3 50.0 %reduce-scatter.6.cloned.1.call-start = ((), (), s32[]{:S(2)}) async-start(), calls=%async_computation.14 | async-start | bytes 1310720 | tf_op jit(solution)/shard_map/reduce_scatter | solution.py:123
  107.4 0.8 copy-start.1
  107.4 1.2 copy-start.6
  109.2 3.5 %copy-start.14 = (f32[2,1024,128]{2,1,0:T(8,128)S(1)}, f32[2,1024,128]{2,1,0:T(8,128)}, u32[]{:S(2)}) copy-start(f32[2,1024,128]{2,1,0:T(8,128)} %get-tuple-element.192) | copy-start | bytes 3145732 | tf_op jit(solution)/shard_map/while
  112.7 1.5 copy-start.2
  113.2 1.0 copy-start.15
  114.2 0.8 copy-start.1
  114.2 1.2 copy-start.6
  115.9 3.5 %copy-start.14 = (f32[2,1024,128]{2,1,0:T(8,128)S(1)}, f32[2,1024,128]{2,1,0:T(8,128)}, u32[]{:S(2)}) copy-start(f32[2,1024,128]{2,1,0:T(8,128)} %get-tuple-element.192) | copy-start | bytes 3145732 | tf_op jit(solution)/shard_map/while
  119.5 1.5 copy-start.2
  120.0 1.0 copy-start.15
  121.0 1.0 copy-start.3
  121.0 1.1 copy-start.10
  121.0 36.4 %copy-start.8 = (bf16[512,512]{1,0:T(8,128)(2,1)S(1)}, bf16[512,512]{1,0:T(8,128)(2,1)}, u32[]{:S(2)}) copy-start(bf16[512,512]{1,0:T(8,128)(2,1)} %copy-done.7) | copy-start | bytes 1572868
  121.0 36.4 %copy-start.17 = (bf16[512,128]{1,0:T(8,128)(2,1)S(1)}, bf16[512,128]{1,0:T(8,128)(2,1)}, u32[]{:S(2)}) copy-start(bf16[512,128]{1,0:T(8,128)(2,1)} %param.20) | copy-start | bytes 393220
  121.0 64.3 %reduce-scatter.8.cloned.1.call-start = ((), (), s32[]{:S(2)}) async-start(), calls=%async_computation.15 | async-start | bytes 1310720 | tf_op jit(solution)/shard_map/reduce_scatter | solution.py:124
  121.1 64.2 %copy-start.5 = (f32[512,512]{1,0:T(8,128)S(1)}, f32[512,512]{1,0:T(8,128)}, u32[]{:S(2)}) copy-start(f32[512,512]{1,0:T(8,128)} %copy-done.4) | copy-start | bytes 3145732
  121.1 64.2 %copy-start.12 = (bf16[512,128]{1,0:T(8,128)(2,1)S(1)}, bf16[512,128]{1,0:T(8,128)(2,1)}, u32[]{:S(2)}) copy-start(bf16[512,128]{1,0:T(8,128)(2,1)} %param.24) | copy-start | bytes 393220
  159.3 27.9 %all-to-all-start.7 = ((bf16[8,64,128]{2,1,0:T(8,128)(2,1)}), bf16[8,64,128]{2,1,0:T(8,128)(2,1)S(1)}, u32[]{:S(2)}, u32[]{:S(2)}) async-start(bf16[8,64,128]{2,1,0:T(8,128)(2,1)} %bitcast.21), calls=%async_computation.8 | async-start | bytes 262144 | tf_op jit(solution)/shard_map/all_to_all | solution.py:133
  187.2 9.1 %all-to-all-start.8 = ((bf16[8,64,128]{2,1,0:T(8,128)(2,1)}), bf16[8,64,128]{2,1,0:T(8,128)(2,1)S(1)}, u32[]{:S(2)}, u32[]{:S(2)}) async-start(bf16[8,64,128]{2,1,0:T(8,128)(2,1)} %bitcast.24), calls=%async_computation.10 | async-start | bytes 262144 | tf_op jit(solution)/shard_map/all_to_all | solution.py:134
Sparse Core Ops, SparseCore 0:
  64.6 23.0 reduce-scatter.9
  89.9 19.1 reduce-scatter.11
  111.4 18.1 reduce-scatter.13
  131.8 25.5 reduce-scatter.5
  159.5 25.7 reduce-scatter.7
where the time goes:
time: 205 us; the launch traced here: 204 us
  waiting for transfers between devices  73.8 us (36%)
  blocking collectives  44.9 us (22%)
  starting transfers between devices  30.5 us (15%)
  matrix products  20.5 us (10%)
  local copies, waits for them, and re-layouts  14.2 us (7%)
  between operations  14.1 us (7%)
  other arithmetic  5.63 us (3%)
    reduce_scatter x1, waiting for transfers between devices, shards(): lax.psum_scatter(value_terms, 'inner', scatter_dimension=0, tiled=True)  22.3 us
    reduce_scatter x1, waiting for transfers between devices, shards(): lax.psum_scatter(key_terms, 'inner', scatter_dimension=0, tiled=True)  22 us
    all_gather x1, blocking collectives, shards(): lax.all_gather(keys, 'inner', axis=0, tiled=True)  19.9 us
    all_gather x1, blocking collectives, shards(): lax.all_gather(values, 'inner', axis=0, tiled=True)  17.1 us
    dot_general x10, matrix products, down_rows(): lax.dot_general(left, right, (((0,), (0,)), ((), ())), preferred_element_...  9.88 us
    all_to_all x1, blocking collectives, shards(): lax.all_to_all(head_grads[0], 'outer', split_axis=0, concat_axis=1, tiled...  7.89 us
    all_to_all x1, starting transfers between devices, shards(): lax.all_to_all(logsum_image, 'outer', split_axis=1, concat_axis=0, tiled=...  5.34 us
    dot_general x10, matrix products, across_rows(): lax.dot_general(left, right, (((1,), (1,)), ((), ())), preferred_element_...  5.31 us
  transfers between devices with their start and end apart: 13, of which 8 were waited for; matrix products, arithmetic and copies ran while one was open for 17% of the time, Pallas kernels for 0%

commit v1 on v0

--- a/solution.py
+++ b/solution.py
@@ -53,7 +53,12 @@
 ):
     queries, keys, values, upstream, attended = (
         lax.all_to_all(query_image, "outer", split_axis=1, concat_axis=0, tiled=True),
-        lax.all_to_all(key_image, "outer", split_axis=1, concat_axis=0, tiled=True),
+        jnp.concatenate(
+            lax.all_to_all(
+                jnp.stack(jnp.split(key_image, lax.axis_size("outer"), axis=1)), "outer", 0, 0
+            ),
+            axis=0,
+        ),
         lax.all_to_all(value_image, "outer", split_axis=1, concat_axis=0, tiled=True),
         lax.all_to_all(upstream_image, "outer", split_axis=1, concat_axis=0, tiled=True),
         lax.all_to_all(attended_image, "outer", split_axis=1, concat_axis=0, tiled=True),

time: 205 us -> 215 us (1.049)
  local copies, waits for them, and re-layouts: 14.2 us -> 24 us
    unnamed x34 -> x39, local copies, waits for them, and re-layouts: 1.37 us -> 10.6 us
  transfers between devices with their start and end apart: 13 -> 13, of which waited for: 8 -> 8; matrix products, arithmetic and copies ran while one was open for 17% -> 21% of each run, Pallas kernels for 0% -> 0%
where the time goes in v1:
time: 215 us; the launch traced here: 213 us
  waiting for transfers between devices  73.8 us (34%)
  blocking collectives  44.9 us (21%)
  starting transfers between devices  30.6 us (14%)
  local copies, waits for them, and re-layouts  24 us (11%)
  matrix products  20.4 us (9%)
  between operations  14.1 us (7%)
  other arithmetic  5.63 us (3%)
    reduce_scatter x1, waiting for transfers between devices, shards(): lax.psum_scatter(value_terms, 'inner', scatter_dimension=0, tiled=True)  22.4 us
    reduce_scatter x1, waiting for transfers between devices, shards(): lax.psum_scatter(key_terms, 'inner', scatter_dimension=0, tiled=True)  22 us
    all_gather x1, blocking collectives, shards(): lax.all_gather(keys, 'inner', axis=0, tiled=True)  19.9 us
    all_gather x1, blocking collectives, shards(): lax.all_gather(values, 'inner', axis=0, tiled=True)  17.1 us
    unnamed x39, local copies, waits for them, and re-layouts  10.6 us
    dot_general x10, matrix products, down_rows(): lax.dot_general(left, right, (((0,), (0,)), ((), ())), preferred_element_...  9.74 us
    all_to_all x1, blocking collectives, shards(): lax.all_to_all(head_grads[0], 'outer', split_axis=0, concat_axis=1, tiled...  7.89 us
    all_to_all x1, starting transfers between devices, shards(): lax.all_to_all(logsum_image, 'outer', split_axis=1, concat_axis=0, tiled=...  5.34 us
  transfers between devices with their start and end apart: 13, of which 8 were waited for; matrix products, arithmetic and copies ran while one was open for 21% of the time, Pallas kernels for 0%

profile of v1, /device:TPU:0, one launch (start us, length us, event | category | flops | bytes accessed | tf_op | source)
XLA Modules:
  0.0 213.4 jit_solution(17294467540245437668)
XLA Ops:
  7.2 5.3 %all-to-all-start.1 = ((f32[64,8,1]{0,2,1:T(1,128)}), f32[64,8,1]{0,2,1:T(1,128)S(1)}, u32[]{:S(2)}, u32[]{:S(2)}) async-start(f32[64,8,1]{0,2,1:T(1,128)} %bitcast.179), calls=%async_computation.1 | async-start | bytes 8192 | tf_op jit(solution)/shard_map/all_to_all | solution.py:66
  12.6 1.3 constant_dynamic-update-slice_fusion.7
  13.9 1.3 constant_dynamic-update-slice_fusion.6
  15.2 1.3 constant_dynamic-update-slice_fusion.5
  16.5 1.3 constant_dynamic-update-slice_fusion.4
  17.9 1.3 constant_dynamic-update-slice_fusion.3
  19.2 1.3 constant_dynamic-update-slice_fusion.2
  20.5 1.3 constant_dynamic-update-slice_fusion.1
  21.8 1.6 copy_bitcast_fusion.6
  23.4 1.6 copy_bitcast_fusion.3
  25.0 1.6 copy_bitcast_fusion.5
  26.6 1.1 multiply_reduce_fusion
  28.5 1.0 fusion.31
  29.4 1.1 fusion.35
  30.6 1.3 constant_dynamic-update-slice_fusion
  31.9 4.2 %all-to-all-start.4 = ((bf16[8,64,128]{2,1,0:T(8,128)(2,1)}), bf16[8,64,128]{2,1,0:T(8,128)(2,1)S(1)}, u32[]{:S(2)}, u32[]{:S(2)}) async-start(bf16[8,64,128]{2,1,0:T(8,128)(2,1)} %constant_dynamic-update-slice_fusion), calls=%async_computation.4 | async-start | bytes 262144 | tf_op jit(solution)/shard_map/all_to_all | solution.py:57
  36.9 4.6 %all-to-all-done.4 = bf16[8,64,128]{2,1,0:T(8,128)(2,1)S(1)} async-done(((bf16[8,64,128]{2,1,0:T(8,128)(2,1)}), bf16[8,64,128]{2,1,0:T(8,128)(2,1)S(1)}, u32[]{:S(2)}, u32[]{:S(2)}) %all-to-all-start.4) | async-done | bytes 131104 | tf_op jit(solution)/shard_map/all_to_all | solution.py:57
  41.6 3.4 %all-to-all-start.5 = ((bf16[64,8,128]{2,0,1:T(8,128)(2,1)}), bf16[64,8,128]{2,0,1:T(8,128)(2,1)S(1)}, u32[]{:S(2)}, u32[]{:S(2)}) async-start(bf16[64,8,128]{2,0,1:T(8,128)(2,1)} %copy_bitcast_fusion.3), calls=%async_computation.5 | async-start | bytes 262144 | tf_op jit(solution)/shard_map/all_to_all | solution.py:62
  45.3 5.1 %all-to-all-done.5 = bf16[64,8,128]{2,0,1:T(8,128)(2,1)S(1)} async-done(((bf16[64,8,128]{2,0,1:T(8,128)(2,1)}), bf16[64,8,128]{2,0,1:T(8,128)(2,1)S(1)}, u32[]{:S(2)}, u32[]{:S(2)}) %all-to-all-start.5) | async-done | bytes 131104 | tf_op jit(solution)/shard_map/all_to_all | solution.py:62
  50.4 3.4 %all-to-all-start.2 = ((bf16[64,8,128]{2,0,1:T(8,128)(2,1)}), bf16[64,8,128]{2,0,1:T(8,128)(2,1)S(1)}, u32[]{:S(2)}, u32[]{:S(2)}) async-start(bf16[64,8,128]{2,0,1:T(8,128)(2,1)} %copy_bitcast_fusion.5), calls=%async_computation.2 | async-start | bytes 262144 | tf_op jit(solution)/shard_map/all_to_all | solution.py:63
  54.1 0.8 copy-done.7
  55.2 4.0 %all-to-all-done.2 = bf16[64,8,128]{2,0,1:T(8,128)(2,1)S(1)} async-done(((bf16[64,8,128]{2,0,1:T(8,128)(2,1)}), bf16[64,8,128]{2,0,1:T(8,128)(2,1)S(1)}, u32[]{:S(2)}, u32[]{:S(2)}) %all-to-all-start.2) | async-done | bytes 131104 | tf_op jit(solution)/shard_map/all_to_all | solution.py:63
  59.2 3.4 %all-to-all-start.3 = ((bf16[64,8,128]{2,0,1:T(8,128)(2,1)}), bf16[64,8,128]{2,0,1:T(8,128)(2,1)S(1)}, u32[]{:S(2)}, u32[]{:S(2)}) async-start(bf16[64,8,128]{2,0,1:T(8,128)(2,1)} %copy_bitcast_fusion.4), calls=%async_computation.3 | async-start | bytes 262144 | tf_op jit(solution)/shard_map/all_to_all | solution.py:64
  62.8 5.2 %all-to-all-done.3 = bf16[64,8,128]{2,0,1:T(8,128)(2,1)S(1)} async-done(((bf16[64,8,128]{2,0,1:T(8,128)(2,1)}), bf16[64,8,128]{2,0,1:T(8,128)(2,1)S(1)}, u32[]{:S(2)}, u32[]{:S(2)}) %all-to-all-start.3) | async-done | bytes 131104 | tf_op jit(solution)/shard_map/all_to_all | solution.py:64
  68.0 3.4 %all-to-all-start = ((bf16[64,8,128]{2,0,1:T(8,128)(2,1)}), bf16[64,8,128]{2,0,1:T(8,128)(2,1)S(1)}, u32[]{:S(2)}, u32[]{:S(2)}) async-start(bf16[64,8,128]{2,0,1:T(8,128)(2,1)} %copy_bitcast_fusion.6), calls=%async_computation | async-start | bytes 262144 | tf_op jit(solution)/shard_map/all_to_all | solution.py:55
  72.2 4.6 %all-to-all-done = bf16[64,8,128]{2,0,1:T(8,128)(2,1)S(1)} async-done(((bf16[64,8,128]{2,0,1:T(8,128)(2,1)}), bf16[64,8,128]{2,0,1:T(8,128)(2,1)S(1)}, u32[]{:S(2)}, u32[]{:S(2)}) %all-to-all-start) | async-done | bytes 131104 | tf_op jit(solution)/shard_map/all_to_all | solution.py:55
  77.5 19.9 %all_gather.6 = bf16[2048,128]{1,0:T(8,128)(2,1)S(1)} all-gather(bf16[512,128]{1,0:T(8,128)(2,1)S(1)} %bitcast.169), channel_id=1, replica_groups=mesh['outer'=8,'inner'=4] {'inner'}, dimensions={0}, use_global_device_ids=true | all-gather | bytes 655360 | tf_op jit(solution)/shard_map/all_gather | solution.py:108
  97.8 0.9 fusion.28
  98.8 17.1 %all_gather.7 = bf16[2048,128]{1,0:T(8,128)(2,1)} all-gather(bf16[512,128]{1,0:T(8,128)(2,1)S(1)} %bitcast.171), channel_id=1, replica_groups=mesh['outer'=8,'inner'=4] {'inner'}, dimensions={0}, use_global_device_ids=true | all-gather | bytes 655360 | tf_op jit(solution)/shard_map/all_gather | solution.py:109
  116.3 0.9 convolution_add_fusion
  117.3 13.6 %while.15 = (s32[]{:T(128)}, f32[512,128]{1,0:T(8,128)}, f32[2,1024,128]{2,1,0:T(8,128)}, f32[2,1024,128]{2,1,0:T(8,128)}, bf16[2,1024,128]{2,1,0:T(8,128)(2,1)S...) while((s32[]{:T(128)}, f32[512,128]{1,0:T(8,128)}, ...), condition=%wide.region_2.3_spmd.clone, body=%wide.region_1.0_spmd.clone.sunk | while | flops 675610624 | bytes 27007272 | solution.py:124
  119.1 2.2 %fusion.116 = f32[512,128]{1,0:T(8,128)} fusion(bf16[1024,512]{1,0:T(8,128)(2,1)S(1)} %multiply_convert_fusion.2, f32[512,128]{1,0:T(8,128)} %get-tuple-element.190, bf16[2,1024,128]{2,1,0:T(8,128)(2,1)} %copy-done.1, s32[]{:T(128)S(6)} %copy.69, pred[]{:T(512)S(6)} %compare.3), kind=kOutput, calls=%fused_computation.9.clone.1 | convolution fusion | flops 134414336 | bytes 1835013 | tf_op jit(solution)/shard_map/while/body/eval_jaxpr/dot_general | solution.py:31
  121.3 1.2 fusion.117
  123.1 1.0 copy-done.15
  125.8 2.3 %fusion.116 = f32[512,128]{1,0:T(8,128)} fusion(bf16[1024,512]{1,0:T(8,128)(2,1)S(1)} %multiply_convert_fusion.2, f32[512,128]{1,0:T(8,128)} %get-tuple-element.190, bf16[2,1024,128]{2,1,0:T(8,128)(2,1)} %copy-done.1, s32[]{:T(128)S(6)} %copy.69, pred[]{:T(512)S(6)} %compare.3), kind=kOutput, calls=%fused_computation.9.clone.1 | convolution fusion | flops 134414336 | bytes 1835013 | tf_op jit(solution)/shard_map/while/body/eval_jaxpr/dot_general | solution.py:31
  128.1 1.2 fusion.117
  129.9 1.0 copy-done.15
  132.3 7.9 %all_to_all.151 = bf16[8,64,128]{2,1,0:T(8,128)(2,1)S(1)} all-to-all(bf16[8,64,128]{2,1,0:T(8,128)(2,1)S(1)} %bitcast.174), channel_id=1, replica_groups=mesh['outer'=8,'inner'=4] {'outer'}, dimensions={0} | all-to-all | bytes 262144 | tf_op jit(solution)/shard_map/all_to_all | solution.py:137
  140.8 1.5 convert_element_type.70
  142.3 1.5 convert_element_type.71
  143.8 1.5 convert_element_type.74
  145.2 22.0 %reduce-scatter.6.cloned.1.call-done = f32[512,128]{1,0:T(8,128)} async-done(((f32[2048,128]{1,0:T(8,128)}), f32[512,128]{1,0:T(8,128)}) %reduce-scatter.6.cloned.1.call-update) | async-done | bytes 262160 | tf_op jit(solution)/shard_map/reduce_scatter | solution.py:128
  167.2 1.9 fusion.36
  169.1 3.7 %all-to-all-start.7 = ((bf16[8,64,128]{2,1,0:T(8,128)(2,1)}), bf16[8,64,128]{2,1,0:T(8,128)(2,1)S(1)}, u32[]{:S(2)}, u32[]{:S(2)}) async-start(bf16[8,64,128]{2,1,0:T(8,128)(2,1)} %bitcast.28), calls=%async_computation.8 | async-start | bytes 262144 | tf_op jit(solution)/shard_map/all_to_all | solution.py:138
  172.8 22.4 %reduce-scatter.8.cloned.1.call-done = f32[512,128]{1,0:T(8,128)} async-done(((f32[2048,128]{1,0:T(8,128)}), f32[512,128]{1,0:T(8,128)}) %reduce-scatter.8.cloned.1.call-update) | async-done | bytes 262160 | tf_op jit(solution)/shard_map/reduce_scatter | solution.py:129
  195.2 1.9 fusion.34
  197.1 3.6 %all-to-all-start.8 = ((bf16[8,64,128]{2,1,0:T(8,128)(2,1)}), bf16[8,64,128]{2,1,0:T(8,128)(2,1)S(1)}, u32[]{:S(2)}, u32[]{:S(2)}) async-start(bf16[8,64,128]{2,1,0:T(8,128)(2,1)} %bitcast.31), calls=%async_computation.10 | async-start | bytes 262144 | tf_op jit(solution)/shard_map/all_to_all | solution.py:139
  201.4 4.8 %all-to-all-done.8 = bf16[8,64,128]{2,1,0:T(8,128)(2,1)S(1)} async-done(((bf16[8,64,128]{2,1,0:T(8,128)(2,1)}), bf16[8,64,128]{2,1,0:T(8,128)(2,1)S(1)}, u32[]{:S(2)}, u32[]{:S(2)}) %all-to-all-start.8) | async-done | bytes 131104 | tf_op jit(solution)/shard_map/all_to_all | solution.py:139
  (94 shorter events, 12.9 us)
Async XLA Ops:
  7.2 21.3 %copy-start = (bf16[512,128]{1,0:T(8,128)(2,1)S(1)}, bf16[512,128]{1,0:T(8,128)(2,1)}, u32[]{:S(2)}) copy-start(bf16[512,128]{1,0:T(8,128)(2,1)} %param.21) | copy-start | bytes 393220
  7.2 37.8 %copy-start.20 = (f32[512,1]{0,1:T(1,128)S(1)}, f32[512,1]{0,1:T(1,128)}, u32[]{:S(2)}) copy-start(f32[512,1]{0,1:T(1,128)} %param.25) | copy-start | bytes 6148
  7.2 37.8 %copy-start.16 = (bf16[512,128]{1,0:T(8,128)(2,1)S(1)}, bf16[512,128]{1,0:T(8,128)(2,1)}, u32[]{:S(2)}) copy-start(bf16[512,128]{1,0:T(8,128)(2,1)} %param.20) | copy-start | bytes 393220
  7.2 28.9 %copy-start.19 = (bf16[64,1024]{1,0:T(8,128)(2,1)S(1)}, bf16[64,1024]{1,0:T(8,128)(2,1)}, u32[]{:S(2)}) copy-start(bf16[64,1024]{1,0:T(8,128)(2,1)} %param.17) | copy-start | bytes 393220
  7.2 24.7 %all-to-all-start.1 = ((f32[64,8,1]{0,2,1:T(1,128)}), f32[64,8,1]{0,2,1:T(1,128)S(1)}, u32[]{:S(2)}, u32[]{:S(2)}) async-start(f32[64,8,1]{0,2,1:T(1,128)} %bitcast.179), calls=%async_computation.1 | async-start | bytes 8192 | tf_op jit(solution)/shard_map/all_to_all | solution.py:66
  23.4 30.4 %copy-start.11 = (bf16[512,128]{1,0:T(8,128)(2,1)S(1)}, bf16[512,128]{1,0:T(8,128)(2,1)}, u32[]{:S(2)}) copy-start(bf16[512,128]{1,0:T(8,128)(2,1)} %param.24) | copy-start | bytes 393220
  31.9 9.7 %all-to-all-start.4 = ((bf16[8,64,128]{2,1,0:T(8,128)(2,1)}), bf16[8,64,128]{2,1,0:T(8,128)(2,1)S(1)}, u32[]{:S(2)}, u32[]{:S(2)}) async-start(bf16[8,64,128]{2,1,0:T(8,128)(2,1)} %constant_dynamic-update-slice_fusion), calls=%async_computation.4 | async-start | bytes 262144 | tf_op jit(solution)/shard_map/all_to_all | solution.py:57
  41.6 8.8 %all-to-all-start.5 = ((bf16[64,8,128]{2,0,1:T(8,128)(2,1)}), bf16[64,8,128]{2,0,1:T(8,128)(2,1)S(1)}, u32[]{:S(2)}, u32[]{:S(2)}) async-start(bf16[64,8,128]{2,0,1:T(8,128)(2,1)} %copy_bitcast_fusion.3), calls=%async_computation.5 | async-start | bytes 262144 | tf_op jit(solution)/shard_map/all_to_all | solution.py:62
  45.3 22.7 %copy-start.4 = (f32[512,512]{0,1:T(8,128)}, f32[512,512]{0,1:T(8,128)S(1)}, u32[]{:S(2)}) copy-start(f32[512,512]{0,1:T(8,128)S(1)} %fusion.24) | copy-start | bytes 3145732
  50.4 8.8 %all-to-all-start.2 = ((bf16[64,8,128]{2,0,1:T(8,128)(2,1)}), bf16[64,8,128]{2,0,1:T(8,128)(2,1)S(1)}, u32[]{:S(2)}, u32[]{:S(2)}) async-start(bf16[64,8,128]{2,0,1:T(8,128)(2,1)} %copy_bitcast_fusion.5), calls=%async_computation.2 | async-start | bytes 262144 | tf_op jit(solution)/shard_map/all_to_all | solution.py:63
  54.1 0.8 copy-start.7
  54.9 22.3 %copy-start.18 = (bf16[512,128]{1,0:T(8,128)(2,1)S(1)}, bf16[512,128]{1,0:T(8,128)(2,1)}, u32[]{:S(2)}) copy-start(bf16[512,128]{1,0:T(8,128)(2,1)} %param.22) | copy-start | bytes 393220
  59.2 8.8 %all-to-all-start.3 = ((bf16[64,8,128]{2,0,1:T(8,128)(2,1)}), bf16[64,8,128]{2,0,1:T(8,128)(2,1)S(1)}, u32[]{:S(2)}, u32[]{:S(2)}) async-start(bf16[64,8,128]{2,0,1:T(8,128)(2,1)} %copy_bitcast_fusion.4), calls=%async_computation.3 | async-start | bytes 262144 | tf_op jit(solution)/shard_map/all_to_all | solution.py:64
  62.8 8.9 %copy-start.13 = (f32[512,128]{1,0:T(8,128)}, f32[512,128]{1,0:T(8,128)S(1)}, u32[]{:S(2)}) copy-start(f32[512,128]{1,0:T(8,128)S(1)} %fusion.39) | copy-start | bytes 786436
  68.0 8.8 %all-to-all-start = ((bf16[64,8,128]{2,0,1:T(8,128)(2,1)}), bf16[64,8,128]{2,0,1:T(8,128)(2,1)S(1)}, u32[]{:S(2)}, u32[]{:S(2)}) async-start(bf16[64,8,128]{2,0,1:T(8,128)(2,1)} %copy_bitcast_fusion.6), calls=%async_computation | async-start | bytes 262144 | tf_op jit(solution)/shard_map/all_to_all | solution.py:55
  71.4 69.4 %reduce-scatter.10.cloned.1.call-start = ((), (), s32[]{:S(2)}) async-start(), calls=%async_computation.16 | async-start | bytes 327680 | tf_op jit(solution)/shard_map/reduce_scatter | solution.py:142
  72.1 70.2 %reduce-scatter.12.cloned.1.call-start = ((), (), s32[]{:S(2)}) async-start(), calls=%async_computation.17 | async-start | bytes 327680 | tf_op jit(solution)/shard_map/reduce_scatter | solution.py:143
  77.5 38.8 %copy-start.9 = (bf16[512,512]{1,0:T(8,128)(2,1)}, bf16[512,512]{1,0:T(8,128)(2,1)S(1)}, u32[]{:S(2)}) copy-start(bf16[512,512]{1,0:T(8,128)(2,1)S(1)} %fusion.27) | copy-start | bytes 1572868
  98.7 45.1 %reduce-scatter.14.cloned.1.call-start = ((), (), s32[]{:S(2)}) async-start(), calls=%async_computation.18 | async-start | bytes 327680 | tf_op jit(solution)/shard_map/reduce_scatter | solution.py:146
  117.2 50.0 %reduce-scatter.6.cloned.1.call-start = ((), (), s32[]{:S(2)}) async-start(), calls=%async_computation.14 | async-start | bytes 1310720 | tf_op jit(solution)/shard_map/reduce_scatter | solution.py:128
  117.3 0.8 copy-start.1
  117.3 1.2 copy-start.6
  119.1 3.5 %copy-start.14 = (f32[2,1024,128]{2,1,0:T(8,128)S(1)}, f32[2,1024,128]{2,1,0:T(8,128)}, u32[]{:S(2)}) copy-start(f32[2,1024,128]{2,1,0:T(8,128)} %get-tuple-element.192) | copy-start | bytes 3145732 | tf_op jit(solution)/shard_map/while
  122.6 1.5 copy-start.2
  123.0 1.0 copy-start.15
  124.0 0.8 copy-start.1
  124.0 1.2 copy-start.6
  125.8 3.5 %copy-start.14 = (f32[2,1024,128]{2,1,0:T(8,128)S(1)}, f32[2,1024,128]{2,1,0:T(8,128)}, u32[]{:S(2)}) copy-start(f32[2,1024,128]{2,1,0:T(8,128)} %get-tuple-element.192) | copy-start | bytes 3145732 | tf_op jit(solution)/shard_map/while
  129.4 1.5 copy-start.2
  129.9 1.0 copy-start.15
  130.9 1.0 copy-start.3
  130.9 1.1 copy-start.10
  130.9 36.3 %copy-start.8 = (bf16[512,512]{0,1:T(8,128)(2,1)S(1)}, bf16[512,512]{0,1:T(8,128)(2,1)}, u32[]{:S(2)}) copy-start(bf16[512,512]{0,1:T(8,128)(2,1)} %copy-done.7) | copy-start | bytes 1572868
  130.9 36.3 %copy-start.17 = (bf16[512,128]{1,0:T(8,128)(2,1)S(1)}, bf16[512,128]{1,0:T(8,128)(2,1)}, u32[]{:S(2)}) copy-start(bf16[512,128]{1,0:T(8,128)(2,1)} %param.20) | copy-start | bytes 393220
  130.9 64.3 %reduce-scatter.8.cloned.1.call-start = ((), (), s32[]{:S(2)}) async-start(), calls=%async_computation.15 | async-start | bytes 1310720 | tf_op jit(solution)/shard_map/reduce_scatter | solution.py:129
  130.9 64.2 %copy-start.5 = (f32[512,512]{0,1:T(8,128)S(1)}, f32[512,512]{0,1:T(8,128)}, u32[]{:S(2)}) copy-start(f32[512,512]{0,1:T(8,128)} %copy-done.4) | copy-start | bytes 3145732
  131.0 64.2 %copy-start.12 = (bf16[512,128]{1,0:T(8,128)(2,1)S(1)}, bf16[512,128]{1,0:T(8,128)(2,1)}, u32[]{:S(2)}) copy-start(bf16[512,128]{1,0:T(8,128)(2,1)} %param.24) | copy-start | bytes 393220
  169.1 28.0 %all-to-all-start.7 = ((bf16[8,64,128]{2,1,0:T(8,128)(2,1)}), bf16[8,64,128]{2,1,0:T(8,128)(2,1)S(1)}, u32[]{:S(2)}, u32[]{:S(2)}) async-start(bf16[8,64,128]{2,1,0:T(8,128)(2,1)} %bitcast.28), calls=%async_computation.8 | async-start | bytes 262144 | tf_op jit(solution)/shard_map/all_to_all | solution.py:138
  197.1 9.1 %all-to-all-start.8 = ((bf16[8,64,128]{2,1,0:T(8,128)(2,1)}), bf16[8,64,128]{2,1,0:T(8,128)(2,1)S(1)}, u32[]{:S(2)}, u32[]{:S(2)}) async-start(bf16[8,64,128]{2,1,0:T(8,128)(2,1)} %bitcast.31), calls=%async_computation.10 | async-start | bytes 262144 | tf_op jit(solution)/shard_map/all_to_all | solution.py:139
Sparse Core Ops, SparseCore 0:
  74.5 23.0 reduce-scatter.9
  99.8 19.1 reduce-scatter.11
  121.3 18.1 reduce-scatter.13
  141.7 25.4 reduce-scatter.5
  169.3 25.7 reduce-scatter.7
